TPU v7x, 32 devices: a whole 2x2x4 slice. The times are simulated.
32 devices in a mesh: ctx: 8 (over z, x), head: 4 (over y, core).
Axes of the slice: x: 2, y: 2, z: 4, core: 2. Of those that a mesh axis runs over, the one named last changes fastest.
Arguments:
- queries: bfloat16 [8192, 512], P('ctx', 'head'), may hold values from -6 to 6
- keys: bfloat16 [8192, 512], P('ctx', 'head'), may hold values from -6 to 6
- values: bfloat16 [8192, 512], P('ctx', 'head'), may hold values from -6 to 6
- write_rates: float32 [4, 8192], P('head', 'ctx'), may hold values from 0 to 2, as said below
- norm_gain: float32 [128], replicated, may hold values from 0.1 to 1.9
- w_out: bfloat16 [512, 2048], P(None, 'head'), may hold values from -0.25 to 0.25
Outputs:
- mixed: bfloat16 [8192, 2048], P('ctx', 'head')
Inputs may be any that keep to these rules, and one draw needn't show every extreme that they name: `write_rates`: every rate lies strictly between 0 and 2.
All inputs are finite; a program needn't handle non-finite values.
Results may differ from a plain program's by a relative error of at most 0.0049.
Values may be sent and summed in bfloat16 or wider, within the bound.
A program may use at most 64 MiB of HBM per device.

v0:
```python
import jax
import jax.numpy as jnp
from jax import lax
from jax.sharding import PartitionSpec as P

HEAD_DIM = 128
GROUP = 128


def passed_along(value, axis, steps):
    count = lax.axis_size(axis)
    leading, last = (max(0, -steps), min(count, count - steps))
    return lax.ppermute(value, axis, [(source, source + steps) for source in range(leading, last)])


def matmul(left, right):
    return jnp.dot(left, right, precision=lax.Precision.HIGHEST, preferred_element_type=jnp.float32)


def unit_rows(matrix):
    wide = matrix.astype(jnp.float32)
    return wide / jnp.sqrt(jnp.sum(wide * wide, axis=-1, keepdims=True) + 1e-06)


def block_parts(query_block, key_block, value_block, rate_block):
    width = key_block.shape[1]
    gram = matmul(key_block, key_block.T)
    lower = jnp.tril(rate_block[:, None] * gram, -1) + jnp.eye(
        key_block.shape[0], dtype=jnp.float32
    )
    stacked = jnp.concatenate(
        [rate_block[:, None] * key_block, rate_block[:, None] * value_block], axis=1
    )
    solved = jax.scipy.linalg.solve_triangular(lower, stacked, lower=True, unit_diagonal=True)
    wy_keys = solved[:, :width]
    wy_values = solved[:, width:]
    transition = jnp.eye(width, dtype=jnp.float32) - matmul(wy_keys.T, key_block)
    offset = matmul(wy_values.T, key_block)
    scores = jnp.tril(matmul(query_block, key_block.T))
    return (wy_keys, wy_values, transition, offset, scores)


def block_output(state, query_block, wy_keys, wy_values, transition, offset, scores):
    result = matmul(query_block, state.T) + matmul(scores, wy_values - matmul(wy_keys, state.T))
    return (result, matmul(state, transition) + offset)


def shards(queries, keys, values, write_rates, norm_gain, w_out):
    length = queries.shape[0]
    blocks = length // GROUP
    query_rows = unit_rows(queries).reshape(blocks, GROUP, HEAD_DIM)
    key_rows = unit_rows(keys).reshape(blocks, GROUP, HEAD_DIM)
    value_rows = values.astype(jnp.float32).reshape(blocks, GROUP, HEAD_DIM)
    rate_rows = write_rates[0].reshape(blocks, GROUP)
    wy_keys, wy_values, transition, offset, scores = jax.vmap(block_parts)(
        query_rows, key_rows, value_rows, rate_rows
    )
    identity_hd = jnp.eye(HEAD_DIM, dtype=jnp.float32)
    zero_state = jnp.zeros((HEAD_DIM, HEAD_DIM), jnp.float32)

    def compose(carry, step):
        return ((matmul(carry[0], step[0]), matmul(carry[1], step[0]) + step[1]), None)

    (device_map, device_offset), unused = lax.scan(
        compose, (identity_hd, zero_state), (transition, offset)
    )

    def relay(step, state):
        return passed_along(matmul(state, device_map) + device_offset, "ctx", 1)

    start_state = lax.fori_loop(0, lax.axis_size("ctx") - 1, relay, zero_state)

    def advance(state, block):
        result, state = block_output(state, *block)
        return (state, result)

    final, outputs = lax.scan(
        advance, start_state, (query_rows, wy_keys, wy_values, transition, offset, scores)
    )
    outputs = outputs.reshape(length, HEAD_DIM)
    normed = (
        outputs * lax.rsqrt(jnp.mean(outputs * outputs, axis=-1, keepdims=True) + 1e-06) * norm_gain
    ).astype(jnp.bfloat16)
    token_rows = lax.all_to_all(normed, "head", split_axis=0, concat_axis=1, tiled=True)
    full_rows = jnp.dot(
        token_rows,
        lax.all_gather(w_out, "head", axis=1, tiled=True),
        preferred_element_type=jnp.float32,
    ).astype(jnp.bfloat16)
    return lax.all_to_all(full_rows, "head", split_axis=1, concat_axis=0, tiled=True)


def solution(mesh):
    return jax.shard_map(
        shards,
        mesh=mesh,
        in_specs=(
            P("ctx", "head"),
            P("ctx", "head"),
            P("ctx", "head"),
            P("head", "ctx"),
            P(),
            P(None, "head"),
        ),
        out_specs=P("ctx", "head"),
        check_vma=False,
    )
```

profile of v0, /device:TPU:24, one launch (start us, length us, event | category | flops | bytes accessed | tf_op | source)
XLA Modules:
  0.0 204.3 jit_solution(2503386418949848491)
XLA Ops:
  7.3 1.2 fusion.36
  8.5 1.2 convert_divide_fusion.1
  9.8 1.9 fusion.31
  11.8 78.6 %custom-call.4 = f32[8,1,128,128]{2,3,1,0:T(8,128)S(1)} custom-call(f32[8,1,128,128]{3,2,1,0:T(8,128)S(1)} %fusion.31), custom_call_target="InvertDiagBlocksLowerTriangular" | custom-call | tf_op jit(solution)/shard_map/vmap(jit(_solve_triangular))/triangular_solve | solution.py:34
  94.8 5.2 %while.40 = (s32[]{:T(128)}, f32[128,128]{0,1:T(8,128)S(1)}, f32[128,128]{0,1:T(8,128)S(1)}, f32[8,128,128]{2,1,0:T(8,128)S(1)}, f32[8,128,128]{1,2,0:T(8,128)S(1)}) while((s32[]{:T(128)}, f32[128,128]{0,1:T(8,128)S(1)}, f32[128,128]{0,1:T(8,128)S(1)}, f32[8,128,128]{2,1,0:T(8,128)S(1)}, ...), condition=%wide.region_2.3_spmd.clone.clone, body=%wide.region_1.0_spmd.clone.sunk.clone | while | flops 50364416 | bytes 721995 | solution.py:64
  100.2 51.2 %while.38 = (s32[]{:T(128)}, f32[128,128]{1,0:T(8,128)S(1)}, f32[128,128]{1,0:T(8,128)S(1)}, f32[128,128]{1,0:T(8,128)S(1)}) while((s32[]{:T(128)}, f32[128,128]{1,0:T(8,128)S(1)}, f32[128,128]{1,0:T(8,128)S(1)}, f32[128,128]{1,0:T(8,128)S(1)}) %tuple.75), condition=%wide.region_4.5_spmd.clone, body=%wide.region_3.4_spmd.sunk.clone | while | flops 25182208 | bytes 524381 | solution.py:71
  100.4 3.4 %collective-permute-start = (f32[128,128]{1,0:T(8,128)S(1)}, f32[128,128]{1,0:T(8,128)S(1)}, u32[]{:S(2)}, u32[]{:S(2)}) collective-permute-start(f32[128,128]{1,0:T(8,128)S(1)} %convolution_add_fusion.4), channel_id=1, source_target_pairs={{0,4},{4,8},{8,12},{12,16},{16,20},{20,24},{24,28},{1,5},{5,9},{9,... | collective-permute-start | bytes 196616 | tf_op jit(solution)/shard_map/while/body/eval_jaxpr/ppermute | solution.py:13
  103.8 3.6 %collective-permute-done = f32[128,128]{1,0:T(8,128)S(1)} collective-permute-done((f32[128,128]{1,0:T(8,128)S(1)}, f32[128,128]{1,0:T(8,128)S(1)}, u32[]{:S(2)}, u32[]{:S(2)}) %collective-permute-start) | collective-permute-done | bytes 65568 | tf_op jit(solution)/shard_map/while/body/eval_jaxpr/ppermute | solution.py:13
  107.7 2.5 %collective-permute-start = (f32[128,128]{1,0:T(8,128)S(1)}, f32[128,128]{1,0:T(8,128)S(1)}, u32[]{:S(2)}, u32[]{:S(2)}) collective-permute-start(f32[128,128]{1,0:T(8,128)S(1)} %convolution_add_fusion.4), channel_id=1, source_target_pairs={{0,4},{4,8},{8,12},{12,16},{16,20},{20,24},{24,28},{1,5},{5,9},{9,... | collective-permute-start | bytes 196616 | tf_op jit(solution)/shard_map/while/body/eval_jaxpr/ppermute | solution.py:13
  110.2 4.5 %collective-permute-done = f32[128,128]{1,0:T(8,128)S(1)} collective-permute-done((f32[128,128]{1,0:T(8,128)S(1)}, f32[128,128]{1,0:T(8,128)S(1)}, u32[]{:S(2)}, u32[]{:S(2)}) %collective-permute-start) | collective-permute-done | bytes 65568 | tf_op jit(solution)/shard_map/while/body/eval_jaxpr/ppermute | solution.py:13
  115.0 1.9 collective-permute-start
  116.9 5.1 %collective-permute-done = f32[128,128]{1,0:T(8,128)S(1)} collective-permute-done((f32[128,128]{1,0:T(8,128)S(1)}, f32[128,128]{1,0:T(8,128)S(1)}, u32[]{:S(2)}, u32[]{:S(2)}) %collective-permute-start) | collective-permute-done | bytes 65568 | tf_op jit(solution)/shard_map/while/body/eval_jaxpr/ppermute | solution.py:13
  122.2 1.9 collective-permute-start
  124.2 5.1 %collective-permute-done = f32[128,128]{1,0:T(8,128)S(1)} collective-permute-done((f32[128,128]{1,0:T(8,128)S(1)}, f32[128,128]{1,0:T(8,128)S(1)}, u32[]{:S(2)}, u32[]{:S(2)}) %collective-permute-start) | collective-permute-done | bytes 65568 | tf_op jit(solution)/shard_map/while/body/eval_jaxpr/ppermute | solution.py:13
  129.5 1.9 collective-permute-start
  131.4 5.4 %collective-permute-done = f32[128,128]{1,0:T(8,128)S(1)} collective-permute-done((f32[128,128]{1,0:T(8,128)S(1)}, f32[128,128]{1,0:T(8,128)S(1)}, u32[]{:S(2)}, u32[]{:S(2)}) %collective-permute-start) | collective-permute-done | bytes 65568 | tf_op jit(solution)/shard_map/while/body/eval_jaxpr/ppermute | solution.py:13
  137.1 1.9 collective-permute-start
  139.0 5.1 %collective-permute-done = f32[128,128]{1,0:T(8,128)S(1)} collective-permute-done((f32[128,128]{1,0:T(8,128)S(1)}, f32[128,128]{1,0:T(8,128)S(1)}, u32[]{:S(2)}, u32[]{:S(2)}) %collective-permute-start) | collective-permute-done | bytes 65568 | tf_op jit(solution)/shard_map/while/body/eval_jaxpr/ppermute | solution.py:13
  144.3 1.9 collective-permute-start
  146.3 5.1 %collective-permute-done = f32[128,128]{1,0:T(8,128)S(1)} collective-permute-done((f32[128,128]{1,0:T(8,128)S(1)}, f32[128,128]{1,0:T(8,128)S(1)}, u32[]{:S(2)}, u32[]{:S(2)}) %collective-permute-start) | collective-permute-done | bytes 65568 | tf_op jit(solution)/shard_map/while/body/eval_jaxpr/ppermute | solution.py:13
  152.0 1.2 convolution_select_fusion
  153.2 14.8 %while.39 = (s32[]{:T(128)}, f32[128,128]{0,1:T(8,128)S(1)}, f32[8,128,128]{2,1,0:T(8,128)S(1)}, f32[8,128,128]{2,1,0:T(8,128)S(1)}, f32[8,128,128]{1,2,0:T(8,12...) while((s32[]{:T(128)}, f32[128,128]{0,1:T(8,128)S(1)}, ...), condition=%wide.region_7.8_spmd.clone, body=%wide.region_6.7_spmd.sunk.clone | while | flops 100712448 | bytes 1117281 | solution.py:77
  153.2 1.1 convolution_subtract_fusion.4
  156.9 1.1 convolution_subtract_fusion.4
  158.8 1.1 convolution_subtract_fusion.4
  160.6 1.1 convolution_subtract_fusion.4
  162.4 1.1 convolution_subtract_fusion.4
  164.3 1.1 convolution_subtract_fusion.4
  166.1 1.1 convolution_subtract_fusion.4
  168.4 8.6 %all_to_all.35 = bf16[4,256,128]{2,1,0:T(8,128)(2,1)S(1)} all-to-all(bf16[4,256,128]{2,1,0:T(8,128)(2,1)S(1)} %fusion.39), channel_id=1, replica_groups=mesh['ctx'=8,'head'=4] {'head'}, dimensions={0} | all-to-all | bytes 524288 | tf_op jit(solution)/shard_map/all_to_all | solution.py:84
  177.2 2.3 %convolution_convert_fusion = bf16[256,2048]{1,0:T(8,128)(2,1)S(1)} fusion(bf16[256,512]{0,1:T(8,128)(2,1)S(1)} %bitcast.150, bf16[512,2048]{1,0:T(8,128)(2,1)} %all-gather.2.cloned.1.call-done), kind=kOutput, calls=%fused_computation.33 | convolution fusion | flops 537395200 | bytes 3407872 | tf_op jit(solution)/shard_map/dot_general | solution.py:85
  179.6 16.9 %all_to_all.36 = bf16[256,4,512]{2,0,1:T(8,128)(2,1)S(1)} all-to-all(bf16[256,4,512]{2,0,1:T(8,128)(2,1)S(1)} %bitcast.144), channel_id=1, replica_groups=mesh['ctx'=8,'head'=4] {'head'}, dimensions={1} | all-to-all | bytes 2097152 | tf_op jit(solution)/shard_map/all_to_all | solution.py:90
  (110 shorter events, 20.6 us)
Async XLA Ops:
  6.5 83.8 %copy-start.2 = (f32[1,1024]{1,0:T(1,128)S(1)}, f32[1,1024]{1,0:T(1,128)}, u32[]{:S(2)}) copy-start(f32[1,1024]{1,0:T(1,128)} %param.15) | copy-start | bytes 12292
  6.5 83.8 %copy-start.1 = (bf16[1024,128]{1,0:T(8,128)(2,1)S(1)}, bf16[1024,128]{1,0:T(8,128)(2,1)}, u32[]{:S(2)}) copy-start(bf16[1024,128]{1,0:T(8,128)(2,1)} %param.14) | copy-start | bytes 786436
  6.5 170.7 %all-gather.2.cloned.1.call-start = ((), (), s32[]{:S(2)}) async-start(), calls=%async_computation.2 | async-start | bytes 2621440 | tf_op jit(solution)/shard_map/all_gather | solution.py:87
  94.8 56.7 %copy-start = (bf16[1024,128]{1,0:T(8,128)(2,1)S(1)}, bf16[1024,128]{1,0:T(8,128)(2,1)}, u32[]{:S(2)}) copy-start(bf16[1024,128]{1,0:T(8,128)(2,1)} %param.12) | copy-start | bytes 786436
  100.4 7.1 %collective-permute-start = (f32[128,128]{1,0:T(8,128)S(1)}, f32[128,128]{1,0:T(8,128)S(1)}, u32[]{:S(2)}, u32[]{:S(2)}) collective-permute-start(f32[128,128]{1,0:T(8,128)S(1)} %convolution_add_fusion.4), channel_id=1, source_target_pairs={{0,4},{4,8},{8,12},{12,16},{16,20},{20,24},{24,28},{1,5},{5,9},{9,... | collective-permute-start | bytes 196616 | tf_op jit(solution)/shard_map/while/body/eval_jaxpr/ppermute | solution.py:13
  107.7 7.1 %collective-permute-start = (f32[128,128]{1,0:T(8,128)S(1)}, f32[128,128]{1,0:T(8,128)S(1)}, u32[]{:S(2)}, u32[]{:S(2)}) collective-permute-start(f32[128,128]{1,0:T(8,128)S(1)} %convolution_add_fusion.4), channel_id=1, source_target_pairs={{0,4},{4,8},{8,12},{12,16},{16,20},{20,24},{24,28},{1,5},{5,9},{9,... | collective-permute-start | bytes 196616 | tf_op jit(solution)/shard_map/while/body/eval_jaxpr/ppermute | solution.py:13
  115.0 7.1 %collective-permute-start = (f32[128,128]{1,0:T(8,128)S(1)}, f32[128,128]{1,0:T(8,128)S(1)}, u32[]{:S(2)}, u32[]{:S(2)}) collective-permute-start(f32[128,128]{1,0:T(8,128)S(1)} %convolution_add_fusion.4), channel_id=1, source_target_pairs={{0,4},{4,8},{8,12},{12,16},{16,20},{20,24},{24,28},{1,5},{5,9},{9,... | collective-permute-start | bytes 196616 | tf_op jit(solution)/shard_map/while/body/eval_jaxpr/ppermute | solution.py:13
  122.2 7.1 %collective-permute-start = (f32[128,128]{1,0:T(8,128)S(1)}, f32[128,128]{1,0:T(8,128)S(1)}, u32[]{:S(2)}, u32[]{:S(2)}) collective-permute-start(f32[128,128]{1,0:T(8,128)S(1)} %convolution_add_fusion.4), channel_id=1, source_target_pairs={{0,4},{4,8},{8,12},{12,16},{16,20},{20,24},{24,28},{1,5},{5,9},{9,... | collective-permute-start | bytes 196616 | tf_op jit(solution)/shard_map/while/body/eval_jaxpr/ppermute | solution.py:13
  129.5 7.4 %collective-permute-start = (f32[128,128]{1,0:T(8,128)S(1)}, f32[128,128]{1,0:T(8,128)S(1)}, u32[]{:S(2)}, u32[]{:S(2)}) collective-permute-start(f32[128,128]{1,0:T(8,128)S(1)} %convolution_add_fusion.4), channel_id=1, source_target_pairs={{0,4},{4,8},{8,12},{12,16},{16,20},{20,24},{24,28},{1,5},{5,9},{9,... | collective-permute-start | bytes 196616 | tf_op jit(solution)/shard_map/while/body/eval_jaxpr/ppermute | solution.py:13
  137.1 7.1 %collective-permute-start = (f32[128,128]{1,0:T(8,128)S(1)}, f32[128,128]{1,0:T(8,128)S(1)}, u32[]{:S(2)}, u32[]{:S(2)}) collective-permute-start(f32[128,128]{1,0:T(8,128)S(1)} %convolution_add_fusion.4), channel_id=1, source_target_pairs={{0,4},{4,8},{8,12},{12,16},{16,20},{20,24},{24,28},{1,5},{5,9},{9,... | collective-permute-start | bytes 196616 | tf_op jit(solution)/shard_map/while/body/eval_jaxpr/ppermute | solution.py:13
  144.3 7.1 %collective-permute-start = (f32[128,128]{1,0:T(8,128)S(1)}, f32[128,128]{1,0:T(8,128)S(1)}, u32[]{:S(2)}, u32[]{:S(2)}) collective-permute-start(f32[128,128]{1,0:T(8,128)S(1)} %convolution_add_fusion.4), channel_id=1, source_target_pairs={{0,4},{4,8},{8,12},{12,16},{16,20},{20,24},{24,28},{1,5},{5,9},{9,... | collective-permute-start | bytes 196616 | tf_op jit(solution)/shard_map/while/body/eval_jaxpr/ppermute | solution.py:13
  153.2 15.0 %copy-start.3 = (f32[128]{0:T(128)S(1)}, f32[128]{0:T(128)}, u32[]{:S(2)}) copy-start(f32[128]{0:T(128)} %param.16) | copy-start | bytes 1540
Sparse Core Ops, SparseCore 0:
  8.9 23.6 all-gather.1
where the time goes:
time: 205 us; the launch traced here: 204 us
  other arithmetic  82.1 us (40%)
  waiting for transfers between devices  34.9 us (17%)
  matrix products  28.9 us (14%)
  blocking collectives  25.5 us (12%)
  starting transfers between devices  15.5 us (8%)
  between operations  13.7 us (7%)
  local copies, waits for them, and re-layouts  2.82 us (1%)
    another operation x3, other arithmetic, block_parts(): jax.scipy.linalg.solve_triangular(lower, stacked, lower=True, unit_diagon...  78.7 us
    ppermute x7, waiting for transfers between devices, passed_along(): lax.ppermute(value, axis, [(source, source + steps) for source in range(l...  34.1 us
    dot_general x59, matrix products, matmul(): jnp.dot(left, right, precision=lax.Precision.HIGHEST, preferred_element_t...  25.6 us
    all_to_all x1, blocking collectives, shards(): lax.all_to_all(full_rows, 'head', split_axis=1, concat_axis=0, tiled=True)  16.9 us
    ppermute x7, starting transfers between devices, passed_along(): lax.ppermute(value, axis, [(source, source + steps) for source in range(l...  15.5 us
    all_to_all x1, blocking collectives, shards(): lax.all_to_all(normed, 'head', split_axis=0, concat_axis=1, tiled=True)  8.6 us
  transfers between devices with their start and end apart: 8, of which 7 were waited for; matrix products, arithmetic and copies ran while one was open for 54% of the time, Pallas kernels for 0%

commit v1 on v0

--- a/solution.py
+++ b/solution.py
@@ -87,7 +87,12 @@
         lax.all_gather(w_out, "head", axis=1, tiled=True),
         preferred_element_type=jnp.float32,
     ).astype(jnp.bfloat16)
-    return lax.all_to_all(full_rows, "head", split_axis=1, concat_axis=0, tiled=True)
+    return jnp.concatenate(
+        lax.all_to_all(
+            jnp.stack(jnp.split(full_rows, lax.axis_size("head"), axis=1)), "head", 0, 0
+        ),
+        axis=0,
+    )
 
 
 def solution(mesh):

time: 205 us -> 205 us (level)
  no operation moved by 1% of the time
where the time goes in v1:
time: 205 us; the launch traced here: 204 us
  other arithmetic  82.2 us (40%)
  waiting for transfers between devices  34.9 us (17%)
  matrix products  28.9 us (14%)
  blocking collectives  25.5 us (12%)
  starting transfers between devices  15.5 us (8%)
  between operations  13.7 us (7%)
  local copies, waits for them, and re-layouts  2.84 us (1%)
    another operation x3, other arithmetic, block_parts(): jax.scipy.linalg.solve_triangular(lower, stacked, lower=True, unit_diagon...  78.7 us
    ppermute x7, waiting for transfers between devices, passed_along(): lax.ppermute(value, axis, [(source, source + steps) for source in range(l...  34.1 us
    dot_general x59, matrix products, matmul(): jnp.dot(left, right, precision=lax.Precision.HIGHEST, preferred_element_t...  25.6 us
    all_to_all x1, blocking collectives, shards(): lax.all_to_all(jnp.stack(jnp.split(full_rows, lax.axis_size('head'), axis...  16.9 us
    ppermute x7, starting transfers between devices, passed_along(): lax.ppermute(value, axis, [(source, source + steps) for source in range(l...  15.5 us
    all_to_all x1, blocking collectives, shards(): lax.all_to_all(normed, 'head', split_axis=0, concat_axis=1, tiled=True)  8.61 us
  transfers between devices with their start and end apart: 8, of which 7 were waited for; matrix products, arithmetic and copies ran while one was open for 54% of the time, Pallas kernels for 0%

profile of v1, /device:TPU:24, one launch (start us, length us, event | category | flops | bytes accessed | tf_op | source)
XLA Modules:
  0.0 204.5 jit_solution(3310499764938694517)
XLA Ops:
  7.3 1.2 fusion.36
  8.5 1.2 convert_divide_fusion.1
  9.8 1.9 fusion.31
  11.8 78.6 %custom-call.4 = f32[8,1,128,128]{2,3,1,0:T(8,128)S(1)} custom-call(f32[8,1,128,128]{3,2,1,0:T(8,128)S(1)} %fusion.31), custom_call_target="InvertDiagBlocksLowerTriangular" | custom-call | tf_op jit(solution)/shard_map/vmap(jit(_solve_triangular))/triangular_solve | solution.py:34
  93.7 1.1 fusion.47
  94.8 5.2 %while.40 = (s32[]{:T(128)}, f32[128,128]{0,1:T(8,128)S(1)}, f32[128,128]{0,1:T(8,128)S(1)}, f32[8,128,128]{2,1,0:T(8,128)S(1)}, f32[8,128,128]{1,2,0:T(8,128)S(1)}) while((s32[]{:T(128)}, f32[128,128]{0,1:T(8,128)S(1)}, f32[128,128]{0,1:T(8,128)S(1)}, f32[8,128,128]{2,1,0:T(8,128)S(1)}, ...), condition=%wide.region_2.3_spmd.clone.clone, body=%wide.region_1.0_spmd.clone.sunk.clone | while | flops 50364416 | bytes 721995 | solution.py:64
  100.2 51.2 %while.38 = (s32[]{:T(128)}, f32[128,128]{1,0:T(8,128)S(1)}, f32[128,128]{1,0:T(8,128)S(1)}, f32[128,128]{1,0:T(8,128)S(1)}) while((s32[]{:T(128)}, f32[128,128]{1,0:T(8,128)S(1)}, f32[128,128]{1,0:T(8,128)S(1)}, f32[128,128]{1,0:T(8,128)S(1)}) %tuple.75), condition=%wide.region_4.5_spmd.clone, body=%wide.region_3.4_spmd.sunk.clone | while | flops 25182208 | bytes 524381 | solution.py:71
  100.4 3.4 %collective-permute-start = (f32[128,128]{1,0:T(8,128)S(1)}, f32[128,128]{1,0:T(8,128)S(1)}, u32[]{:S(2)}, u32[]{:S(2)}) collective-permute-start(f32[128,128]{1,0:T(8,128)S(1)} %convolution_add_fusion.4), channel_id=1, source_target_pairs={{0,4},{4,8},{8,12},{12,16},{16,20},{20,24},{24,28},{1,5},{5,9},{9,... | collective-permute-start | bytes 196616 | tf_op jit(solution)/shard_map/while/body/eval_jaxpr/ppermute | solution.py:13
  103.8 3.6 %collective-permute-done = f32[128,128]{1,0:T(8,128)S(1)} collective-permute-done((f32[128,128]{1,0:T(8,128)S(1)}, f32[128,128]{1,0:T(8,128)S(1)}, u32[]{:S(2)}, u32[]{:S(2)}) %collective-permute-start) | collective-permute-done | bytes 65568 | tf_op jit(solution)/shard_map/while/body/eval_jaxpr/ppermute | solution.py:13
  107.7 2.5 %collective-permute-start = (f32[128,128]{1,0:T(8,128)S(1)}, f32[128,128]{1,0:T(8,128)S(1)}, u32[]{:S(2)}, u32[]{:S(2)}) collective-permute-start(f32[128,128]{1,0:T(8,128)S(1)} %convolution_add_fusion.4), channel_id=1, source_target_pairs={{0,4},{4,8},{8,12},{12,16},{16,20},{20,24},{24,28},{1,5},{5,9},{9,... | collective-permute-start | bytes 196616 | tf_op jit(solution)/shard_map/while/body/eval_jaxpr/ppermute | solution.py:13
  110.2 4.5 %collective-permute-done = f32[128,128]{1,0:T(8,128)S(1)} collective-permute-done((f32[128,128]{1,0:T(8,128)S(1)}, f32[128,128]{1,0:T(8,128)S(1)}, u32[]{:S(2)}, u32[]{:S(2)}) %collective-permute-start) | collective-permute-done | bytes 65568 | tf_op jit(solution)/shard_map/while/body/eval_jaxpr/ppermute | solution.py:13
  115.0 1.9 collective-permute-start
  116.9 5.1 %collective-permute-done = f32[128,128]{1,0:T(8,128)S(1)} collective-permute-done((f32[128,128]{1,0:T(8,128)S(1)}, f32[128,128]{1,0:T(8,128)S(1)}, u32[]{:S(2)}, u32[]{:S(2)}) %collective-permute-start) | collective-permute-done | bytes 65568 | tf_op jit(solution)/shard_map/while/body/eval_jaxpr/ppermute | solution.py:13
  122.2 1.9 collective-permute-start
  124.2 5.1 %collective-permute-done = f32[128,128]{1,0:T(8,128)S(1)} collective-permute-done((f32[128,128]{1,0:T(8,128)S(1)}, f32[128,128]{1,0:T(8,128)S(1)}, u32[]{:S(2)}, u32[]{:S(2)}) %collective-permute-start) | collective-permute-done | bytes 65568 | tf_op jit(solution)/shard_map/while/body/eval_jaxpr/ppermute | solution.py:13
  129.5 1.9 collective-permute-start
  131.4 5.4 %collective-permute-done = f32[128,128]{1,0:T(8,128)S(1)} collective-permute-done((f32[128,128]{1,0:T(8,128)S(1)}, f32[128,128]{1,0:T(8,128)S(1)}, u32[]{:S(2)}, u32[]{:S(2)}) %collective-permute-start) | collective-permute-done | bytes 65568 | tf_op jit(solution)/shard_map/while/body/eval_jaxpr/ppermute | solution.py:13
  137.1 1.9 collective-permute-start
  139.0 5.1 %collective-permute-done = f32[128,128]{1,0:T(8,128)S(1)} collective-permute-done((f32[128,128]{1,0:T(8,128)S(1)}, f32[128,128]{1,0:T(8,128)S(1)}, u32[]{:S(2)}, u32[]{:S(2)}) %collective-permute-start) | collective-permute-done | bytes 65568 | tf_op jit(solution)/shard_map/while/body/eval_jaxpr/ppermute | solution.py:13
  144.4 1.9 collective-permute-start
  146.3 5.1 %collective-permute-done = f32[128,128]{1,0:T(8,128)S(1)} collective-permute-done((f32[128,128]{1,0:T(8,128)S(1)}, f32[128,128]{1,0:T(8,128)S(1)}, u32[]{:S(2)}, u32[]{:S(2)}) %collective-permute-start) | collective-permute-done | bytes 65568 | tf_op jit(solution)/shard_map/while/body/eval_jaxpr/ppermute | solution.py:13
  152.0 1.2 convolution_select_fusion
  153.2 14.8 %while.39 = (s32[]{:T(128)}, f32[128,128]{0,1:T(8,128)S(1)}, f32[8,128,128]{2,1,0:T(8,128)S(1)}, f32[8,128,128]{2,1,0:T(8,128)S(1)}, f32[8,128,128]{1,2,0:T(8,12...) while((s32[]{:T(128)}, f32[128,128]{0,1:T(8,128)S(1)}, ...), condition=%wide.region_7.8_spmd.clone, body=%wide.region_6.7_spmd.sunk.clone | while | flops 100712448 | bytes 1117281 | solution.py:77
  153.2 1.1 convolution_subtract_fusion.4
  155.1 1.1 convolution_subtract_fusion.4
  156.9 1.1 convolution_subtract_fusion.4
  160.6 1.1 convolution_subtract_fusion.4
  162.5 1.1 convolution_subtract_fusion.4
  164.3 1.1 convolution_subtract_fusion.4
  168.4 8.6 %all_to_all.21 = bf16[4,256,128]{2,1,0:T(8,128)(2,1)S(1)} all-to-all(bf16[4,256,128]{2,1,0:T(8,128)(2,1)S(1)} %fusion.39), channel_id=1, replica_groups=mesh['ctx'=8,'head'=4] {'head'}, dimensions={0} | all-to-all | bytes 524288 | tf_op jit(solution)/shard_map/all_to_all | solution.py:84
  177.2 2.3 %convolution_convert_fusion = bf16[256,2048]{1,0:T(8,128)(2,1)S(1)} fusion(bf16[256,512]{0,1:T(8,128)(2,1)S(1)} %bitcast.150, bf16[512,2048]{1,0:T(8,128)(2,1)} %all-gather.2.cloned.1.call-done), kind=kOutput, calls=%fused_computation.33 | convolution fusion | flops 537395200 | bytes 3407872 | tf_op jit(solution)/shard_map/dot_general | solution.py:85
  179.8 16.9 %all_to_all.22 = bf16[4,256,512]{2,1,0:T(8,128)(2,1)S(1)} all-to-all(bf16[4,256,512]{2,1,0:T(8,128)(2,1)S(1)} %pad_maximum_fusion), channel_id=1, replica_groups=mesh['ctx'=8,'head'=4] {'head'}, dimensions={0} | all-to-all | bytes 2097152 | tf_op jit(solution)/shard_map/all_to_all | solution.py:91
  (111 shorter events, 20.8 us)
Async XLA Ops:
  6.5 83.8 %copy-start.2 = (f32[1,1024]{1,0:T(1,128)S(1)}, f32[1,1024]{1,0:T(1,128)}, u32[]{:S(2)}) copy-start(f32[1,1024]{1,0:T(1,128)} %param.15) | copy-start | bytes 12292
  6.5 83.8 %copy-start.1 = (bf16[1024,128]{1,0:T(8,128)(2,1)S(1)}, bf16[1024,128]{1,0:T(8,128)(2,1)}, u32[]{:S(2)}) copy-start(bf16[1024,128]{1,0:T(8,128)(2,1)} %param.14) | copy-start | bytes 786436
  6.5 170.7 %all-gather.2.cloned.1.call-start = ((), (), s32[]{:S(2)}) async-start(), calls=%async_computation.2 | async-start | bytes 2621440 | tf_op jit(solution)/shard_map/all_gather | solution.py:87
  94.8 56.7 %copy-start = (bf16[1024,128]{1,0:T(8,128)(2,1)S(1)}, bf16[1024,128]{1,0:T(8,128)(2,1)}, u32[]{:S(2)}) copy-start(bf16[1024,128]{1,0:T(8,128)(2,1)} %param.12) | copy-start | bytes 786436
  100.4 7.1 %collective-permute-start = (f32[128,128]{1,0:T(8,128)S(1)}, f32[128,128]{1,0:T(8,128)S(1)}, u32[]{:S(2)}, u32[]{:S(2)}) collective-permute-start(f32[128,128]{1,0:T(8,128)S(1)} %convolution_add_fusion.4), channel_id=1, source_target_pairs={{0,4},{4,8},{8,12},{12,16},{16,20},{20,24},{24,28},{1,5},{5,9},{9,... | collective-permute-start | bytes 196616 | tf_op jit(solution)/shard_map/while/body/eval_jaxpr/ppermute | solution.py:13
  107.7 7.1 %collective-permute-start = (f32[128,128]{1,0:T(8,128)S(1)}, f32[128,128]{1,0:T(8,128)S(1)}, u32[]{:S(2)}, u32[]{:S(2)}) collective-permute-start(f32[128,128]{1,0:T(8,128)S(1)} %convolution_add_fusion.4), channel_id=1, source_target_pairs={{0,4},{4,8},{8,12},{12,16},{16,20},{20,24},{24,28},{1,5},{5,9},{9,... | collective-permute-start | bytes 196616 | tf_op jit(solution)/shard_map/while/body/eval_jaxpr/ppermute | solution.py:13
  115.0 7.1 %collective-permute-start = (f32[128,128]{1,0:T(8,128)S(1)}, f32[128,128]{1,0:T(8,128)S(1)}, u32[]{:S(2)}, u32[]{:S(2)}) collective-permute-start(f32[128,128]{1,0:T(8,128)S(1)} %convolution_add_fusion.4), channel_id=1, source_target_pairs={{0,4},{4,8},{8,12},{12,16},{16,20},{20,24},{24,28},{1,5},{5,9},{9,... | collective-permute-start | bytes 196616 | tf_op jit(solution)/shard_map/while/body/eval_jaxpr/ppermute | solution.py:13
  122.2 7.1 %collective-permute-start = (f32[128,128]{1,0:T(8,128)S(1)}, f32[128,128]{1,0:T(8,128)S(1)}, u32[]{:S(2)}, u32[]{:S(2)}) collective-permute-start(f32[128,128]{1,0:T(8,128)S(1)} %convolution_add_fusion.4), channel_id=1, source_target_pairs={{0,4},{4,8},{8,12},{12,16},{16,20},{20,24},{24,28},{1,5},{5,9},{9,... | collective-permute-start | bytes 196616 | tf_op jit(solution)/shard_map/while/body/eval_jaxpr/ppermute | solution.py:13
  129.5 7.4 %collective-permute-start = (f32[128,128]{1,0:T(8,128)S(1)}, f32[128,128]{1,0:T(8,128)S(1)}, u32[]{:S(2)}, u32[]{:S(2)}) collective-permute-start(f32[128,128]{1,0:T(8,128)S(1)} %convolution_add_fusion.4), channel_id=1, source_target_pairs={{0,4},{4,8},{8,12},{12,16},{16,20},{20,24},{24,28},{1,5},{5,9},{9,... | collective-permute-start | bytes 196616 | tf_op jit(solution)/shard_map/while/body/eval_jaxpr/ppermute | solution.py:13
  137.1 7.1 %collective-permute-start = (f32[128,128]{1,0:T(8,128)S(1)}, f32[128,128]{1,0:T(8,128)S(1)}, u32[]{:S(2)}, u32[]{:S(2)}) collective-permute-start(f32[128,128]{1,0:T(8,128)S(1)} %convolution_add_fusion.4), channel_id=1, source_target_pairs={{0,4},{4,8},{8,12},{12,16},{16,20},{20,24},{24,28},{1,5},{5,9},{9,... | collective-permute-start | bytes 196616 | tf_op jit(solution)/shard_map/while/body/eval_jaxpr/ppermute | solution.py:13
  144.4 7.1 %collective-permute-start = (f32[128,128]{1,0:T(8,128)S(1)}, f32[128,128]{1,0:T(8,128)S(1)}, u32[]{:S(2)}, u32[]{:S(2)}) collective-permute-start(f32[128,128]{1,0:T(8,128)S(1)} %convolution_add_fusion.4), channel_id=1, source_target_pairs={{0,4},{4,8},{8,12},{12,16},{16,20},{20,24},{24,28},{1,5},{5,9},{9,... | collective-permute-start | bytes 196616 | tf_op jit(solution)/shard_map/while/body/eval_jaxpr/ppermute | solution.py:13
  153.2 15.0 %copy-start.3 = (f32[128]{0:T(128)S(1)}, f32[128]{0:T(128)}, u32[]{:S(2)}) copy-start(f32[128]{0:T(128)} %param.16) | copy-start | bytes 1540
Sparse Core Ops, SparseCore 0:
  8.9 23.6 all-gather.1
